TPU v7x, 32 devices: a whole 2x2x4 slice. The times are simulated.
32 devices in a mesh: groups: 2 (over y), gx: 4 (over z), gy: 2 (over x), gz: 2 (over core).
Axes of the slice: x: 2, y: 2, z: 4, core: 2. Of those that a mesh axis runs over, the one named last changes fastest.
Arguments:
- coords: float32 [8, 8, 16, 3, 128], P(('groups', 'gx'), 'gy', 'gz'), parts along dimension 0, may hold values from 0 to 1.1
- charges: float32 [8, 8, 16, 128], P(('groups', 'gx'), 'gy', 'gz'), parts along dimension 0, may hold values from -2 to 2
- atom_types: int32 [8, 8, 16, 128], P(('groups', 'gx'), 'gy', 'gz'), parts along dimension 0, may hold values from 0 to 63
- counts: int32 [8, 8, 16], P(('groups', 'gx'), 'gy', 'gz'), parts along dimension 0, may hold values from 64 to 128
- c6_table: float32 [64, 64], replicated, may hold values from 0.0001 to 0.001
- c12_table: float32 [64, 64], replicated, may hold values from 1e-08 to 1e-07
Outputs:
- forces: float32 [8, 8, 16, 3, 128], P(('groups', 'gx'), 'gy', 'gz'), parts along dimension 0
- energy: float32 [2], P('groups'), parts along dimension 0
There are 2 independent parts, one for each index of `groups`. A program takes and returns all parts, laid end to end along the dimension named above; an argument that names none is the same for every part. Nothing has to cross between parts.
All inputs are finite; a program needn't handle non-finite values.
Results may differ from a plain program's by a relative error of at most 0.0003.
Values sent between devices are 32-bit elements; how exact they have to be, the bound alone decides.
A program may use at most 64 MiB of HBM per device.

v0:
```python
import functools

import jax
import jax.numpy as jnp
from jax import lax
from jax.experimental import pallas as pl
from jax.experimental.pallas import tpu as pltpu
from jax.sharding import PartitionSpec as P

CELL_EDGE = 1.1
SOFTEN = 0.09
ENERGY_UNIT = 0.1
EDGE_V = 1.0 / (1.0 + SOFTEN)
E0 = EDGE_V**0.5
E3 = EDGE_V**3
UNROLL = 4
GROUPS = (
    ((1, -1, -1, 3), (1, 0, -1, 3), (0, 0, 0, 2)),
    ((1, 1, -1, 3), (0, 1, -1, 3)),
)
SELF_ROW = 6


def shifted(block, axis, distance):
    n = lax.axis_size(axis)
    route = [((i - distance) % n, i) for i in range(n)]
    return lax.ppermute(block, axis, route)


def from_both(first, last, axis):
    if lax.axis_size(axis) == 2:
        both = shifted(jnp.stack([first, last]), axis, 1)
        return both[0], both[1]
    return shifted(first, axis, -1), shifted(last, axis, 1)


def pair_kernel(cx, cy, cz, nt, scal_ref, type_ref, count_ref, ext_ref, c6_ref, c12_ref,
                force_ref, energy_ref, tcell, table, fa):
    ey = cy + 2
    ez = cz + 2
    slots = 128
    force_ref[...] = jnp.zeros_like(force_ref)
    fa[...] = jnp.zeros_like(fa)
    table[...] = jnp.zeros_like(table)
    c6 = c6_ref[...]
    c12 = c12_ref[...]
    c6 = (0.5 * ENERGY_UNIT) * (c6 + c6.T)
    c12 = (0.5 * ENERGY_UNIT) * (c12 + c12.T)
    both = jnp.concatenate([c12, c6], axis=0)
    high = both.astype(jnp.bfloat16)
    low = (both - high.astype(jnp.float32)).astype(jnp.bfloat16)
    left = jnp.concatenate([high, low], axis=1)
    ids = lax.broadcasted_iota(jnp.int32, (nt, slots), 0).astype(jnp.float32)

    def table_of(xy, carry):
        for z in range(ez):
            row = ext_ref[4, xy, z : z + 1, :]
            hot = (ids == row).astype(jnp.float32).astype(jnp.bfloat16)
            tcell[xy, z] = jnp.dot(
                left, jnp.concatenate([hot, hot], axis=0), preferred_element_type=jnp.float32
            )
        return carry

    lax.fori_loop(1, (cx + 1) * ey, table_of, 0)

    rows = lax.broadcasted_iota(jnp.int32, (8, slots), 0)
    lanes = lax.broadcasted_iota(jnp.int32, (8, slots), 1)
    self_lane = jnp.where(rows == SELF_ROW, lanes, slots)
    ones = jnp.ones((8, slots), jnp.float32)

    def cell(c, e_sum):
        x = c // (cy * cz)
        y = (c // cz) % cy
        z = c % cz
        b_rows = []
        for g, runs in enumerate(GROUPS):
            comps = [[], [], [], []]
            r = 0
            for ox, oy, oz, length in runs:
                xy = (x + ox) * ey + y + 1 + oy
                z0 = z + 1 + oz
                for k in range(4):
                    comps[k].append(ext_ref[k, xy, pl.ds(z0, length), :])
                for j in range(length):
                    t = tcell.at[xy, z0 + j]
                    table[pl.ds(8 * g + r, nt, stride=32), :] = t[:nt, :]
                    table[pl.ds(16 + 8 * g + r, nt, stride=32), :] = t[nt:, :]
                    r += 1
            if r < 8:
                for k in range(4):
                    comps[k].append(jnp.zeros((8 - r, slots), jnp.float32))
            full = [jnp.concatenate(p, axis=0) for p in comps]
            for k in range(3):
                off = jnp.zeros((8, slots), jnp.float32)
                r = 0
                for ox, oy, oz, length in runs:
                    for j in range(length):
                        o = (ox, oy, oz + j)[k]
                        if o:
                            off = jnp.where(rows == r, jnp.float32(o * CELL_EDGE), off)
                        r += 1
                full[k] = full[k] + off
            full[3] = full[3] * ENERGY_UNIT
            b_rows.append(full)
        n_atoms = count_ref[c]

        def atoms(step, carry):
            acc = [list(carry[0:3]), list(carry[3:6])]
            e_acc = carry[6]
            for uu in range(UNROLL):
                i = step * UNROLL + uu
                at = c * (4 * slots) + i
                xi = scal_ref[at]
                yi = scal_ref[at + slots]
                zi = scal_ref[at + 2 * slots]
                qi = scal_ref[at + 3 * slots]
                ti = pl.multiple_of(type_ref[c * slots + i] * 32, 32)
                mine = None
                for g in range(2):
                    bx, by, bz, bq = b_rows[g]
                    c12p = table[pl.ds(ti + 8 * g, 8), :]
                    c6p = table[pl.ds(ti + 16 + 8 * g, 8), :]
                    dx = bx - xi
                    dy = by - yi
                    dz = bz - zi
                    t = dx * dx + dy * dy + (dz * dz + SOFTEN)
                    s = lax.rsqrt(t)
                    v = s * s
                    z3 = v * v * v
                    w = jnp.maximum((1.0 + SOFTEN) - t, 0.0)
                    if g == 0:
                        w = jnp.where(self_lane > i, w, 0.0)
                    qq = bq * qi
                    cz12 = c12p * z3
                    y1 = cz12 - c6p
                    u = qq * (s - E0) + (z3 - E3) * (y1 + c12p * E3)
                    h = qq * s + (z3 * 6.0) * (y1 + cz12)
                    uw = u * w
                    e_acc = e_acc + uw * w
                    gg = w * (v * h * w) + 4.0 * uw
                    f = [gg * dx, gg * dy, gg * dz]
                    acc[g] = [p + q for p, q in zip(acc[g], f)]
                    mine = f if mine is None else [p + q for p, q in zip(mine, f)]
                for k in range(3):
                    fa[k, pl.ds(pl.multiple_of(i * 8, 8), 8), :] = mine[k]
            return (*acc[0], *acc[1], e_acc)

        zero = jnp.zeros((8, slots), jnp.float32)
        out = lax.fori_loop(0, (n_atoms + UNROLL - 1) // UNROLL, atoms, (zero,) * 6 + (e_sum,))
        for g, runs in enumerate(GROUPS):
            r = 0
            for ox, oy, oz, length in runs:
                xy = (x + ox) * ey + y + 1 + oy
                for k in range(3):
                    force_ref[k, xy, pl.ds(z + 1 + oz, length), :] += out[3 * g + k][r : r + length]
                r += length
        occupied = lax.broadcasted_iota(jnp.int32, (1, slots), 1) < n_atoms
        for k in range(3):
            total = fa[k, pl.ds(0, slots, stride=8), :]
            for s in range(1, 8):
                total = total + fa[k, pl.ds(s, slots, stride=8), :]
            summed = lax.dot_general(
                ones, total, (((1,), (1,)), ((), ())),
                precision=lax.Precision.HIGHEST, preferred_element_type=jnp.float32,
            )[:1]
            force_ref[k, x * ey + y + 1, pl.ds(z + 1, 1), :] -= jnp.where(occupied, summed, 0.0)
        return out[6]

    e = lax.fori_loop(0, cx * cy * cz, cell, jnp.zeros((8, slots), jnp.float32))
    energy_ref[...] = e


def on_device(coords, charges, atom_types, counts, c6_table, c12_table):
    cx, cy, cz, _, slots = coords.shape
    nt = c6_table.shape[0]
    occ = jnp.arange(slots, dtype=jnp.int32) < counts[..., None]
    charge = jnp.where(occ, charges, 0.0)
    kind = jnp.where(occ, atom_types, nt)
    local = jnp.concatenate(
        [jnp.moveaxis(coords, 3, 0), charge[None], kind.astype(jnp.float32)[None]], axis=0
    )
    scal = jnp.concatenate([coords, charge[..., None, :]], axis=3).reshape(-1)
    up = shifted(local[:, :1], "gx", -1)
    ext = jnp.concatenate([local, up], axis=1)
    above, below = from_both(ext[:, :, :1], ext[:, :, -1:], "gy")
    ext = jnp.concatenate([below, ext, above], axis=2)
    above, below = from_both(ext[:, :, :, :1], ext[:, :, :, -1:], "gz")
    ext = jnp.concatenate([below, ext, above], axis=3)
    ex, ey, ez = cx + 1, cy + 2, cz + 2
    vm = pl.BlockSpec(memory_space=pltpu.VMEM)
    sm = pl.BlockSpec(memory_space=pltpu.SMEM)
    forces, energy = pl.pallas_call(
        functools.partial(pair_kernel, cx, cy, cz, nt),
        out_shape=(
            jax.ShapeDtypeStruct((3, ex * ey, ez, slots), jnp.float32),
            jax.ShapeDtypeStruct((8, slots), jnp.float32),
        ),
        in_specs=[sm, sm, sm, vm, vm, vm],
        out_specs=(vm, vm),
        scratch_shapes=[
            pltpu.VMEM((ex * ey, ez, 2 * nt, slots), jnp.float32),
            pltpu.VMEM(((nt + 1) * 32, slots), jnp.float32),
            pltpu.VMEM((3, slots * 8, slots), jnp.float32),
        ],
        compiler_params=pltpu.CompilerParams(vmem_limit_bytes=48 * 2**20),
    )(scal, kind.reshape(-1), counts.reshape(-1), ext.reshape(5, ex * ey, ez, slots), c6_table, c12_table)
    energies = lax.all_gather(jnp.sum(energy).reshape(1), ("gx", "gy", "gz"), tiled=True)
    forces = forces.reshape(3, ex, ey, ez, slots)
    low, high = from_both(forces[:, :, :, :1], forces[:, :, :, -1:], "gz")
    forces = forces[:, :, :, 1:-1].at[:, :, :, -1:].add(low).at[:, :, :, :1].add(high)
    low, high = from_both(forces[:, :, :1], forces[:, :, -1:], "gy")
    forces = forces[:, :, 1:-1].at[:, :, -1:].add(low).at[:, :, :1].add(high)
    back = shifted(forces[:, cx:], "gx", 1)
    forces = forces[:, :cx].at[:, :1].add(back)
    return jnp.moveaxis(forces, 0, 3), jnp.sum(energies).reshape(1)


def solution(mesh):
    return jax.shard_map(
        on_device,
        mesh=mesh,
        in_specs=(
            P(("groups", "gx"), "gy", "gz", None, None),
            P(("groups", "gx"), "gy", "gz", None),
            P(("groups", "gx"), "gy", "gz", None),
            P(("groups", "gx"), "gy", "gz"),
            P(),
            P(),
        ),
        out_specs=(P(("groups", "gx"), "gy", "gz", None, None), P("groups")),
        check_vma=False,
    )
```

profile of v0, /device:TPU:0, one launch (start us, length us, event | category | flops | bytes accessed | tf_op | source)
XLA Modules:
  0.0 163.2 jit_solution(17711007900380171537)
XLA Ops:
  0.6 0.8 fusion.11
  1.5 0.8 fusion.10
  2.4 5.1 %collective-permute-start = (f32[5,1,4,8,128]{4,1,0,3,2:T(1,128)S(1)}, f32[5,1,4,8,128]{4,1,0,3,2:T(1,128)S(1)}, u32[]{:S(2)}, u32[]{:S(2)}) collective-permute-start(f32[5,1,4,8,128]{4,1,0,3,2:T(1,128)S(1)} %pad_maximum_fusion.3), channel_id=1, source_target_pairs={{4,0},{8,4},{12,8},{0,12},{5,1},{9,5},{13,9},{1,13},{6,2},{10,6},{... | collective-permute-start | bytes 245768 | tf_op jit(solution)/shard_map/ppermute | solution.py:27
  7.5 2.1 %collective-permute-done = f32[5,1,4,8,128]{4,1,0,3,2:T(1,128)S(1)} collective-permute-done((f32[5,1,4,8,128]{4,1,0,3,2:T(1,128)S(1)}, f32[5,1,4,8,128]{4,1,0,3,2:T(1,128)S(1)}, u32[]{:S(2)}, u32[]{:S(2)}) %collective-permute-start) | collective-permute-done | bytes 81952 | tf_op jit(solution)/shard_map/ppermute | solution.py:27
  9.6 0.2 pad_maximum_fusion.2
  9.8 1.6 collective-permute-start.1
  11.5 2.8 %collective-permute-done.1 = f32[2,5,2,1,8,128]{5,2,1,4,3,0:T(2,128)S(1)} collective-permute-done((f32[2,5,2,1,8,128]{5,2,1,4,3,0:T(2,128)S(1)}, f32[2,5,2,1,8,128]{5,2,1,4,3,0:T(2,128)S(1)}, u32[]{:S(2)}, u32[]{:S(2)}) %collective-permute-start.1) | collective-permute-done | bytes 81952 | tf_op jit(solution)/shard_map/ppermute | solution.py:27
  14.3 0.2 pad_maximum_fusion.1
  14.8 1.2 collective-permute-done.2
  16.0 0.1 pad_maximum_fusion.ext_ref
  16.1 0.6 copy-done
  16.8 99.5 %shard_map.82 = (f32[3,12,10,128]{3,2,1,0:T(8,128)S(1)}, f32[8,128]{1,0:T(8,128)S(1)}) custom-call(f32[16384]{0:T(1024)S(1)} %bitcast.76, s32[4096]{0:T(1024)S(1)} %get-tuple-element.90.type_ref, s32[32]{0:T(128)S(1)} %reshape.248.count_ref, f32[5,12,10,128]{3,2,1,0:T(8,128)S(1)} %pad_maximum_fusion.ext_ref, f32[64,64]{1,0:T(8,128)S(1)} %copy-done, ...), custom_call_target="tpu_custom_call" | custom-call | tf_op jit(solution)/shard_map/pallas_call | solution.py:192
  116.4 2.3 %collective-permute-start.3 = (f32[2,3,2,6,1,128]{5,2,3,1,4,0:T(2,128)S(1)}, f32[2,3,2,6,1,128]{5,2,3,1,4,0:T(2,128)S(1)}, u32[]{:S(2)}, u32[]{:S(2)}) collective-permute-start(f32[2,3,2,6,1,128]{5,2,3,1,4,0:T(2,128)S(1)} %pad_maximum_fusion.8), channel_id=1, source_target_pairs={{1,0},{0,1},{3,2},{2,3},{5,4},{4,5},{7,6},{6,7},{9,8},{8,9},{11,10... | collective-permute-start | bytes 110600 | tf_op jit(solution)/shard_map/ppermute | solution.py:27
  118.8 0.8 collective-permute-done.3
  119.7 3.6 %collective-permute-start.4 = (f32[2,3,2,1,8,128]{5,2,1,4,3,0:T(2,128)S(1)}, f32[2,3,2,1,8,128]{5,2,1,4,3,0:T(2,128)S(1)}, u32[]{:S(2)}, u32[]{:S(2)}) collective-permute-start(f32[2,3,2,1,8,128]{5,2,1,4,3,0:T(2,128)S(1)} %pad_maximum_fusion.7), channel_id=1, source_target_pairs={{2,0},{0,2},{3,1},{1,3},{6,4},{4,6},{7,5},{5,7},{10,8},{8,10},{11,... | collective-permute-start | bytes 147464 | tf_op jit(solution)/shard_map/ppermute | solution.py:27
  123.4 2.0 %collective-permute-done.4 = f32[2,3,2,1,8,128]{5,2,1,4,3,0:T(2,128)S(1)} collective-permute-done((f32[2,3,2,1,8,128]{5,2,1,4,3,0:T(2,128)S(1)}, f32[2,3,2,1,8,128]{5,2,1,4,3,0:T(2,128)S(1)}, u32[]{:S(2)}, u32[]{:S(2)}) %collective-permute-start.4) | collective-permute-done | bytes 49184 | tf_op jit(solution)/shard_map/ppermute | solution.py:27
  125.5 0.5 collective-permute-start.5
  126.1 0.7 copy-done.5
  126.7 0.6 dynamic-slice.33
  127.3 0.6 reduce_sum.18
  127.9 1.4 dynamic-update-slice.14
  129.3 32.6 %all-reduce = f32[16]{0:T(128)S(1)} all-reduce(f32[16]{0:T(128)S(1)} %dynamic-update-slice.14), channel_id=1, replica_groups=mesh['groups'=2,'gx'=4,'gy'=2,'gz'=2] {'gx','gy','gz'}, use_global_device_ids=true, to_apply=%add | all-reduce | flops 16 | bytes 128
  161.9 0.6 reduce_sum.19
  162.6 0.6 copy.41
  (43 shorter events, 1.1 us)
Async XLA Ops:
  0.6 1.6 %copy-start.2 = (f32[1,4,8,3,128]{4,2,3,1,0:T(8,128)S(1)}, f32[1,4,8,3,128]{4,2,3,1,0:T(8,128)}, u32[]{:S(2)}) copy-start(f32[1,4,8,3,128]{4,2,3,1,0:T(8,128)} %param.18) | copy-start | bytes 147460
  0.6 0.8 copy-start.4
  2.4 7.2 %collective-permute-start = (f32[5,1,4,8,128]{4,1,0,3,2:T(1,128)S(1)}, f32[5,1,4,8,128]{4,1,0,3,2:T(1,128)S(1)}, u32[]{:S(2)}, u32[]{:S(2)}) collective-permute-start(f32[5,1,4,8,128]{4,1,0,3,2:T(1,128)S(1)} %pad_maximum_fusion.3), channel_id=1, source_target_pairs={{4,0},{8,4},{12,8},{0,12},{5,1},{9,5},{13,9},{1,13},{6,2},{10,6},{... | collective-permute-start | bytes 245768 | tf_op jit(solution)/shard_map/ppermute | solution.py:27
  9.8 1.6 copy-start.3
  9.8 4.5 %collective-permute-start.1 = (f32[2,5,2,1,8,128]{5,2,1,4,3,0:T(2,128)S(1)}, f32[2,5,2,1,8,128]{5,2,1,4,3,0:T(2,128)S(1)}, u32[]{:S(2)}, u32[]{:S(2)}) collective-permute-start(f32[2,5,2,1,8,128]{5,2,1,4,3,0:T(2,128)S(1)} %pad_maximum_fusion.4), channel_id=1, source_target_pairs={{2,0},{0,2},{3,1},{1,3},{6,4},{4,6},{7,5},{5,7},{10,8},{8,10},{11,... | collective-permute-start | bytes 245768 | tf_op jit(solution)/shard_map/ppermute | solution.py:27
  14.6 1.3 collective-permute-start.2
  16.0 0.8 copy-start
  16.0 0.8 copy-start.1
  116.4 3.2 %collective-permute-start.3 = (f32[2,3,2,6,1,128]{5,2,3,1,4,0:T(2,128)S(1)}, f32[2,3,2,6,1,128]{5,2,3,1,4,0:T(2,128)S(1)}, u32[]{:S(2)}, u32[]{:S(2)}) collective-permute-start(f32[2,3,2,6,1,128]{5,2,3,1,4,0:T(2,128)S(1)} %pad_maximum_fusion.8), channel_id=1, source_target_pairs={{1,0},{0,1},{3,2},{2,3},{5,4},{4,5},{7,6},{6,7},{9,8},{8,9},{11,10... | collective-permute-start | bytes 110600 | tf_op jit(solution)/shard_map/ppermute | solution.py:27
  119.7 5.7 %collective-permute-start.4 = (f32[2,3,2,1,8,128]{5,2,1,4,3,0:T(2,128)S(1)}, f32[2,3,2,1,8,128]{5,2,1,4,3,0:T(2,128)S(1)}, u32[]{:S(2)}, u32[]{:S(2)}) collective-permute-start(f32[2,3,2,1,8,128]{5,2,1,4,3,0:T(2,128)S(1)} %pad_maximum_fusion.7), channel_id=1, source_target_pairs={{2,0},{0,2},{3,1},{1,3},{6,4},{4,6},{7,5},{5,7},{10,8},{8,10},{11,... | collective-permute-start | bytes 147464 | tf_op jit(solution)/shard_map/ppermute | solution.py:27
  125.5 37.0 %collective-permute-start.5 = (f32[3,1,4,8,128]{4,1,0,3,2:T(1,128)S(1)}, f32[3,1,4,8,128]{4,1,0,3,2:T(1,128)S(1)}, u32[]{:S(2)}, u32[]{:S(2)}) collective-permute-start(f32[3,1,4,8,128]{4,1,0,3,2:T(1,128)S(1)} %slice.274), channel_id=1, source_target_pairs={{12,0},{0,4},{4,8},{8,12},{13,1},{1,5},{5,9},{9,13},{14,2},{2,6},{... | collective-permute-start | bytes 147464 | tf_op jit(solution)/shard_map/ppermute | solution.py:27
  126.1 0.7 copy-start.5
where the time goes:
time: 165 us; the launch traced here: 163 us
  Pallas kernels  99.5 us (60%)
  blocking collectives  32.6 us (20%)
  starting transfers between devices  13.2 us (8%)
  waiting for transfers between devices  8.8 us (5%)
  local copies, waits for them, and re-layouts  4.49 us (3%)
  other arithmetic  3.65 us (2%)
    pallas_call x1, Pallas kernels, on_device(): pl.pallas_call(functools.partial(pair_kernel, cx, cy, cz, nt), out_shape=...  99.5 us
    unnamed x1, blocking collectives  32.6 us
    ppermute x6, starting transfers between devices, shifted(): return lax.ppermute(block, axis, route)  13.2 us
    ppermute x6, waiting for transfers between devices, shifted(): return lax.ppermute(block, axis, route)  8.8 us
    unnamed x19, local copies, waits for them, and re-layouts  4.11 us
  transfers between devices with their start and end apart: 6, of which 5 were waited for; matrix products, arithmetic and copies ran while one was open for 2% of the time, Pallas kernels for 0%

commit v1 on v0

--- a/solution.py
+++ b/solution.py
@@ -13,7 +13,7 @@
 EDGE_V = 1.0 / (1.0 + SOFTEN)
 E0 = EDGE_V**0.5
 E3 = EDGE_V**3
-UNROLL = 4
+UNROLL = 8
 GROUPS = (
     ((1, -1, -1, 3), (1, 0, -1, 3), (0, 0, 0, 2)),
     ((1, 1, -1, 3), (0, 1, -1, 3)),
@@ -34,8 +34,25 @@
     return shifted(first, axis, -1), shifted(last, axis, 1)
 
 
+def ring_sum(value, axis):
+    total = value
+    for distance in range(1, lax.axis_size(axis)):
+        total = total + shifted(value, axis, distance)
+    return total
+
+
+def returned(first, last, energy, axis):
+    if lax.axis_size(axis) != 2:
+        return (*from_both(first, last, axis), ring_sum(energy, axis))
+    slots = energy.shape[-1]
+    rows = jnp.stack([first, last]).reshape(-1, slots)
+    got = shifted(jnp.concatenate([rows, energy]), axis, 1)
+    both = got[:-1].reshape(2, *first.shape)
+    return both[0], both[1], energy + got[-1:]
+
+
 def pair_kernel(cx, cy, cz, nt, scal_ref, type_ref, count_ref, ext_ref, c6_ref, c12_ref,
-                force_ref, energy_ref, tcell, table, fa):
+                force_ref, energy_ref, tcell, table, fa, columns, flat):
     ey = cy + 2
     ez = cz + 2
     slots = 128
@@ -66,7 +83,8 @@
     rows = lax.broadcasted_iota(jnp.int32, (8, slots), 0)
     lanes = lax.broadcasted_iota(jnp.int32, (8, slots), 1)
     self_lane = jnp.where(rows == SELF_ROW, lanes, slots)
-    ones = jnp.ones((8, slots), jnp.float32)
+    wide_lanes = lax.broadcasted_iota(jnp.int32, (slots, slots), 1)
+    columns[...] = jnp.zeros_like(columns)
 
     def cell(c, e_sum):
         x = c // (cy * cz)
@@ -154,20 +172,27 @@
                 for k in range(3):
                     force_ref[k, xy, pl.ds(z + 1 + oz, length), :] += out[3 * g + k][r : r + length]
                 r += length
-        occupied = lax.broadcasted_iota(jnp.int32, (1, slots), 1) < n_atoms
+        mine_lane = wide_lanes == c % slots
         for k in range(3):
             total = fa[k, pl.ds(0, slots, stride=8), :]
             for s in range(1, 8):
                 total = total + fa[k, pl.ds(s, slots, stride=8), :]
-            summed = lax.dot_general(
-                ones, total, (((1,), (1,)), ((), ())),
-                precision=lax.Precision.HIGHEST, preferred_element_type=jnp.float32,
-            )[:1]
-            force_ref[k, x * ey + y + 1, pl.ds(z + 1, 1), :] -= jnp.where(occupied, summed, 0.0)
+            summed = jnp.sum(total, axis=1, keepdims=True)
+            columns[k, c // slots] = jnp.where(mine_lane, summed, columns[k, c // slots])
         return out[6]
 
-    e = lax.fori_loop(0, cx * cy * cz, cell, jnp.zeros((8, slots), jnp.float32))
+    n_cells = cx * cy * cz
+    e = lax.fori_loop(0, n_cells, cell, jnp.zeros((8, slots), jnp.float32))
     energy_ref[...] = e
+    for k in range(3):
+        for part in range(columns.shape[1]):
+            flat[pl.ds(part * slots, slots), :] = columns[k, part].T
+        for xy in range(cx * cy):
+            at = (xy // cy) * ey + xy % cy + 1
+            for z in range(cz):
+                c = xy * cz + z
+                occupied = lanes[:1] < count_ref[c]
+                force_ref[k, at, z + 1 : z + 2, :] -= jnp.where(occupied, flat[c : c + 1, :], 0.0)
 
 
 def on_device(coords, charges, atom_types, counts, c6_table, c12_table):
@@ -186,6 +211,7 @@
     ext = jnp.concatenate([below, ext, above], axis=2)
     above, below = from_both(ext[:, :, :, :1], ext[:, :, :, -1:], "gz")
     ext = jnp.concatenate([below, ext, above], axis=3)
+    parts = (cx * cy * cz + slots - 1) // slots
     ex, ey, ez = cx + 1, cy + 2, cz + 2
     vm = pl.BlockSpec(memory_space=pltpu.VMEM)
     sm = pl.BlockSpec(memory_space=pltpu.SMEM)
@@ -201,18 +227,21 @@
             pltpu.VMEM((ex * ey, ez, 2 * nt, slots), jnp.float32),
             pltpu.VMEM(((nt + 1) * 32, slots), jnp.float32),
             pltpu.VMEM((3, slots * 8, slots), jnp.float32),
+            pltpu.VMEM((3, parts, slots, slots), jnp.float32),
+            pltpu.VMEM((parts * slots, slots), jnp.float32),
         ],
         compiler_params=pltpu.CompilerParams(vmem_limit_bytes=48 * 2**20),
     )(scal, kind.reshape(-1), counts.reshape(-1), ext.reshape(5, ex * ey, ez, slots), c6_table, c12_table)
-    energies = lax.all_gather(jnp.sum(energy).reshape(1), ("gx", "gy", "gz"), tiled=True)
+    energy = jnp.sum(energy, axis=0, keepdims=True)
     forces = forces.reshape(3, ex, ey, ez, slots)
-    low, high = from_both(forces[:, :, :, :1], forces[:, :, :, -1:], "gz")
+    low, high, energy = returned(forces[:, :, :, :1], forces[:, :, :, -1:], energy, "gz")
     forces = forces[:, :, :, 1:-1].at[:, :, :, -1:].add(low).at[:, :, :, :1].add(high)
-    low, high = from_both(forces[:, :, :1], forces[:, :, -1:], "gy")
+    low, high, energy = returned(forces[:, :, :1], forces[:, :, -1:], energy, "gy")
     forces = forces[:, :, 1:-1].at[:, :, -1:].add(low).at[:, :, :1].add(high)
     back = shifted(forces[:, cx:], "gx", 1)
     forces = forces[:, :cx].at[:, :1].add(back)
-    return jnp.moveaxis(forces, 0, 3), jnp.sum(energies).reshape(1)
+    energy = jnp.sum(ring_sum(energy, "gx"))
+    return jnp.moveaxis(forces, 0, 3), energy.reshape(1)
 
 
 def solution(mesh):

time: 165 us -> 128 us (0.78)
  blocking collectives: 32.6 us -> 0 us
  Pallas kernels: 99.5 us -> 92.6 us
  waiting for transfers between devices: 8.8 us -> 13.1 us
  local copies, waits for them, and re-layouts: 4.49 us -> 2.04 us
  starting transfers between devices: 13.2 us -> 15.6 us
    unnamed x1 -> x0, blocking collectives: 32.6 us -> none
    pallas_call x1, Pallas kernels: 99.5 us -> 92.6 us  [on_device(): pl.pallas_call(functools.partial(pair_kernel, cx, cy, cz, nt), out_shape=...]
    ppermute x6 -> x9, waiting for transfers between devices: 8.8 us -> 13.1 us  [shifted(): return lax.ppermute(block, axis, route)]
    unnamed x19 -> x13, local copies, waits for them, and re-layouts: 4.11 us -> 1.4 us
    ppermute x6 -> x9, starting transfers between devices: 13.2 us -> 15.6 us  [shifted(): return lax.ppermute(block, axis, route)]
  transfers between devices with their start and end apart: 6 -> 9, of which waited for: 5 -> 7; matrix products, arithmetic and copies ran while one was open for 2% -> 1% of each run, Pallas kernels for 0% -> 0%
where the time goes in v1:
time: 128 us; the launch traced here: 127 us
  Pallas kernels  92.6 us (72%)
  starting transfers between devices  15.6 us (12%)
  waiting for transfers between devices  13.1 us (10%)
  other arithmetic  3.08 us (2%)
  local copies, waits for them, and re-layouts  2.04 us (2%)
    pallas_call x1, Pallas kernels, on_device(): pl.pallas_call(functools.partial(pair_kernel, cx, cy, cz, nt), out_shape=...  92.6 us
    ppermute x9, starting transfers between devices, shifted(): return lax.ppermute(block, axis, route)  15.6 us
    ppermute x9, waiting for transfers between devices, shifted(): return lax.ppermute(block, axis, route)  13.1 us
  transfers between devices with their start and end apart: 9, of which 7 were waited for; matrix products, arithmetic and copies ran while one was open for 1% of the time, Pallas kernels for 0%

profile of v1, /device:TPU:0, one launch (start us, length us, event | category | flops | bytes accessed | tf_op | source)
XLA Modules:
  0.0 127.4 jit_solution(653881805035439581)
XLA Ops:
  0.6 0.8 fusion.5
  1.5 0.8 fusion.4
  2.4 5.1 %collective-permute-start = (f32[5,1,4,8,128]{4,1,0,3,2:T(1,128)S(1)}, f32[5,1,4,8,128]{4,1,0,3,2:T(1,128)S(1)}, u32[]{:S(2)}, u32[]{:S(2)}) collective-permute-start(f32[5,1,4,8,128]{4,1,0,3,2:T(1,128)S(1)} %pad_maximum_fusion.3), channel_id=1, source_target_pairs={{4,0},{8,4},{12,8},{0,12},{5,1},{9,5},{13,9},{1,13},{6,2},{10,6},{... | collective-permute-start | bytes 245768 | tf_op jit(solution)/shard_map/ppermute | solution.py:27
  7.5 2.1 %collective-permute-done = f32[5,1,4,8,128]{4,1,0,3,2:T(1,128)S(1)} collective-permute-done((f32[5,1,4,8,128]{4,1,0,3,2:T(1,128)S(1)}, f32[5,1,4,8,128]{4,1,0,3,2:T(1,128)S(1)}, u32[]{:S(2)}, u32[]{:S(2)}) %collective-permute-start) | collective-permute-done | bytes 81952 | tf_op jit(solution)/shard_map/ppermute | solution.py:27
  9.6 0.2 pad_maximum_fusion.2
  9.8 1.6 %collective-permute-start.1 = (f32[2,5,2,1,8,128]{5,2,1,4,3,0:T(2,128)S(1)}, f32[2,5,2,1,8,128]{5,2,1,4,3,0:T(2,128)S(1)}, u32[]{:S(2)}, u32[]{:S(2)}) collective-permute-start(f32[2,5,2,1,8,128]{5,2,1,4,3,0:T(2,128)S(1)} %pad_maximum_fusion.4), channel_id=1, source_target_pairs={{2,0},{0,2},{3,1},{1,3},{6,4},{4,6},{7,5},{5,7},{10,8},{8,10},{11,... | collective-permute-start | bytes 245768 | tf_op jit(solution)/shard_map/ppermute | solution.py:27
  11.5 2.8 %collective-permute-done.1 = f32[2,5,2,1,8,128]{5,2,1,4,3,0:T(2,128)S(1)} collective-permute-done((f32[2,5,2,1,8,128]{5,2,1,4,3,0:T(2,128)S(1)}, f32[2,5,2,1,8,128]{5,2,1,4,3,0:T(2,128)S(1)}, u32[]{:S(2)}, u32[]{:S(2)}) %collective-permute-start.1) | collective-permute-done | bytes 81952 | tf_op jit(solution)/shard_map/ppermute | solution.py:27
  14.3 0.2 pad_maximum_fusion.1
  14.8 1.2 collective-permute-done.2
  16.1 0.6 copy-done
  16.8 92.6 %shard_map.82 = (f32[3,12,10,128]{3,2,1,0:T(8,128)S(1)}, f32[8,128]{1,0:T(8,128)S(1)}) custom-call(f32[16384]{0:T(1024)S(1)} %bitcast.50, s32[4096]{0:T(1024)S(1)} %get-tuple-element.94.type_ref, s32[32]{0:T(128)S(1)} %reshape.261.count_ref, f32[5,12,10,128]{3,2,1,0:T(8,128)S(1)} %pad_maximum_fusion.ext_ref, f32[64,64]{1,0:T(8,128)S(1)} %copy-done, ...), custom_call_target="tpu_custom_call" | custom-call | tf_op jit(solution)/shard_map/pallas_call | solution.py:218
  109.5 0.3 collective-permute-start.3
  110.0 0.9 collective-permute-done.3
  111.0 1.2 collective-permute-start.4
  112.3 2.9 %collective-permute-done.4 = f32[97,128]{1,0:T(8,128)S(1)} collective-permute-done((f32[97,128]{1,0:T(8,128)S(1)}, f32[97,128]{1,0:T(8,128)S(1)}, u32[]{:S(2)}, u32[]{:S(2)}) %collective-permute-start.4) | collective-permute-done | bytes 49696 | tf_op jit(solution)/shard_map/ppermute | solution.py:27
  115.2 1.4 %collective-permute-start.6 = (f32[1,128]{1,0:T(1,128)S(1)}, f32[1,128]{1,0:T(1,128)S(1)}, u32[]{:S(2)}, u32[]{:S(2)}) collective-permute-start(f32[1,128]{1,0:T(1,128)S(1)} %slice_add_fusion.4), channel_id=1, source_target_pairs={{12,0},{0,4},{4,8},{8,12},{13,1},{1,5},{5,9},{9,13},{14,2},{2,6},{... | collective-permute-start | bytes 1544 | tf_op jit(solution)/shard_map/ppermute | solution.py:27
  116.6 3.8 %collective-permute-start.7 = (f32[1,128]{1,0:T(1,128)S(1)}, f32[1,128]{1,0:T(1,128)S(1)}, u32[]{:S(2)}, u32[]{:S(2)}) collective-permute-start(f32[1,128]{1,0:T(1,128)S(1)} %slice_add_fusion.4), channel_id=1, source_target_pairs={{8,0},{12,4},{0,8},{4,12},{9,1},{13,5},{1,9},{5,13},{10,2},{14,6},... | collective-permute-start | bytes 1544 | tf_op jit(solution)/shard_map/ppermute | solution.py:27
  120.5 0.1 scatter-add.16
  120.7 0.1 scatter-add.19
  120.8 2.1 %collective-permute-start.5 = (f32[3,1,4,8,128]{4,2,1,0,3:T(4,128)S(1)}, f32[3,1,4,8,128]{4,2,1,0,3:T(4,128)S(1)}, u32[]{:S(2)}, u32[]{:S(2)}) collective-permute-start(f32[3,1,4,8,128]{4,2,1,0,3:T(4,128)S(1)} %slice.293), channel_id=1, source_target_pairs={{12,0},{0,4},{4,8},{8,12},{13,1},{1,5},{5,9},{9,13},{14,2},{2,6},{... | collective-permute-start | bytes 147464 | tf_op jit(solution)/shard_map/ppermute | solution.py:27
  122.9 1.1 collective-permute-done.8
  124.0 0.6 add_reduce_fusion
  124.6 2.2 %collective-permute-done.5 = f32[3,1,4,8,128]{4,2,1,0,3:T(4,128)S(1)} collective-permute-done((f32[3,1,4,8,128]{4,2,1,0,3:T(4,128)S(1)}, f32[3,1,4,8,128]{4,2,1,0,3:T(4,128)S(1)}, u32[]{:S(2)}, u32[]{:S(2)}) %collective-permute-start.5) | collective-permute-done | bytes 49184 | tf_op jit(solution)/shard_map/ppermute | solution.py:27
  126.8 0.6 copy.41
  (52 shorter events, 1.1 us)
Async XLA Ops:
  0.6 1.6 %copy-start.2 = (f32[1,4,8,3,128]{4,2,3,1,0:T(8,128)S(1)}, f32[1,4,8,3,128]{4,2,3,1,0:T(8,128)}, u32[]{:S(2)}) copy-start(f32[1,4,8,3,128]{4,2,3,1,0:T(8,128)} %param.18) | copy-start | bytes 147460
  0.6 0.8 copy-start.4
  2.4 7.2 %collective-permute-start = (f32[5,1,4,8,128]{4,1,0,3,2:T(1,128)S(1)}, f32[5,1,4,8,128]{4,1,0,3,2:T(1,128)S(1)}, u32[]{:S(2)}, u32[]{:S(2)}) collective-permute-start(f32[5,1,4,8,128]{4,1,0,3,2:T(1,128)S(1)} %pad_maximum_fusion.3), channel_id=1, source_target_pairs={{4,0},{8,4},{12,8},{0,12},{5,1},{9,5},{13,9},{1,13},{6,2},{10,6},{... | collective-permute-start | bytes 245768 | tf_op jit(solution)/shard_map/ppermute | solution.py:27
  9.8 1.6 %copy-start.3 = (f32[1,4,8,128]{3,2,1,0:T(8,128)S(1)}, f32[1,4,8,128]{3,2,1,0:T(8,128)}, u32[]{:S(2)}) copy-start(f32[1,4,8,128]{3,2,1,0:T(8,128)} %param.19) | copy-start | bytes 49156
  9.8 4.5 %collective-permute-start.1 = (f32[2,5,2,1,8,128]{5,2,1,4,3,0:T(2,128)S(1)}, f32[2,5,2,1,8,128]{5,2,1,4,3,0:T(2,128)S(1)}, u32[]{:S(2)}, u32[]{:S(2)}) collective-permute-start(f32[2,5,2,1,8,128]{5,2,1,4,3,0:T(2,128)S(1)} %pad_maximum_fusion.4), channel_id=1, source_target_pairs={{2,0},{0,2},{3,1},{1,3},{6,4},{4,6},{7,5},{5,7},{10,8},{8,10},{11,... | collective-permute-start | bytes 245768 | tf_op jit(solution)/shard_map/ppermute | solution.py:27
  14.6 1.3 %collective-permute-start.2 = (f32[2,5,2,6,1,128]{5,2,3,1,4,0:T(2,128)S(1)}, f32[2,5,2,6,1,128]{5,2,3,1,4,0:T(2,128)S(1)}, u32[]{:S(2)}, u32[]{:S(2)}) collective-permute-start(f32[2,5,2,6,1,128]{5,2,3,1,4,0:T(2,128)S(1)} %pad_maximum_fusion.6), channel_id=1, source_target_pairs={{1,0},{0,1},{3,2},{2,3},{5,4},{4,5},{7,6},{6,7},{9,8},{8,9},{11,10... | collective-permute-start | bytes 184328 | tf_op jit(solution)/shard_map/ppermute | solution.py:27
  16.0 0.8 copy-start
  16.0 0.8 copy-start.1
  109.5 1.3 %collective-permute-start.3 = (f32[73,128]{1,0:T(8,128)S(1)}, f32[73,128]{1,0:T(8,128)S(1)}, u32[]{:S(2)}, u32[]{:S(2)}) collective-permute-start(f32[73,128]{1,0:T(8,128)S(1)} %pad_maximum_fusion.9), channel_id=1, source_target_pairs={{1,0},{0,1},{3,2},{2,3},{5,4},{4,5},{7,6},{6,7},{9,8},{8,9},{11,10... | collective-permute-start | bytes 112136 | tf_op jit(solution)/shard_map/ppermute | solution.py:27
  111.0 4.2 %collective-permute-start.4 = (f32[97,128]{1,0:T(8,128)S(1)}, f32[97,128]{1,0:T(8,128)S(1)}, u32[]{:S(2)}, u32[]{:S(2)}) collective-permute-start(f32[97,128]{1,0:T(8,128)S(1)} %pad_maximum_fusion.7), channel_id=1, source_target_pairs={{2,0},{0,2},{3,1},{1,3},{6,4},{4,6},{7,5},{5,7},{10,8},{8,10},{11,... | collective-permute-start | bytes 149000 | tf_op jit(solution)/shard_map/ppermute | solution.py:27
  115.2 7.7 %collective-permute-start.6 = (f32[1,128]{1,0:T(1,128)S(1)}, f32[1,128]{1,0:T(1,128)S(1)}, u32[]{:S(2)}, u32[]{:S(2)}) collective-permute-start(f32[1,128]{1,0:T(1,128)S(1)} %slice_add_fusion.4), channel_id=1, source_target_pairs={{12,0},{0,4},{4,8},{8,12},{13,1},{1,5},{5,9},{9,13},{14,2},{2,6},{... | collective-permute-start | bytes 1544 | tf_op jit(solution)/shard_map/ppermute | solution.py:27
  116.6 6.3 %collective-permute-start.7 = (f32[1,128]{1,0:T(1,128)S(1)}, f32[1,128]{1,0:T(1,128)S(1)}, u32[]{:S(2)}, u32[]{:S(2)}) collective-permute-start(f32[1,128]{1,0:T(1,128)S(1)} %slice_add_fusion.4), channel_id=1, source_target_pairs={{8,0},{12,4},{0,8},{4,12},{9,1},{13,5},{1,9},{5,13},{10,2},{14,6},... | collective-permute-start | bytes 1544 | tf_op jit(solution)/shard_map/ppermute | solution.py:27
  120.4 3.6 %collective-permute-start.8 = (f32[1,128]{1,0:T(1,128)S(1)}, f32[1,128]{1,0:T(1,128)S(1)}, u32[]{:S(2)}, u32[]{:S(2)}) collective-permute-start(f32[1,128]{1,0:T(1,128)S(1)} %slice_add_fusion.4), channel_id=1, source_target_pairs={{4,0},{8,4},{12,8},{0,12},{5,1},{9,5},{13,9},{1,13},{6,2},{10,6},{... | collective-permute-start | bytes 1544 | tf_op jit(solution)/shard_map/ppermute | solution.py:27
  120.8 5.9 %collective-permute-start.5 = (f32[3,1,4,8,128]{4,2,1,0,3:T(4,128)S(1)}, f32[3,1,4,8,128]{4,2,1,0,3:T(4,128)S(1)}, u32[]{:S(2)}, u32[]{:S(2)}) collective-permute-start(f32[3,1,4,8,128]{4,2,1,0,3:T(4,128)S(1)} %slice.293), channel_id=1, source_target_pairs={{12,0},{0,4},{4,8},{8,12},{13,1},{1,5},{5,9},{9,13},{14,2},{2,6},{... | collective-permute-start | bytes 147464 | tf_op jit(solution)/shard_map/ppermute | solution.py:27

commit v2 on v1

--- a/solution.py
+++ b/solution.py
@@ -52,12 +52,13 @@
 
 
 def pair_kernel(cx, cy, cz, nt, scal_ref, type_ref, count_ref, ext_ref, c6_ref, c12_ref,
-                force_ref, energy_ref, tcell, table, fa, columns, flat):
+                force_ref, energy_ref, tcell, table, fa, fb, columns, flat):
     ey = cy + 2
     ez = cz + 2
     slots = 128
     force_ref[...] = jnp.zeros_like(force_ref)
     fa[...] = jnp.zeros_like(fa)
+    fb[...] = jnp.zeros_like(fb)
     table[...] = jnp.zeros_like(table)
     c6 = c6_ref[...]
     c12 = c12_ref[...]
@@ -101,8 +102,8 @@
                     comps[k].append(ext_ref[k, xy, pl.ds(z0, length), :])
                 for j in range(length):
                     t = tcell.at[xy, z0 + j]
-                    table[pl.ds(8 * g + r, nt, stride=32), :] = t[:nt, :]
-                    table[pl.ds(16 + 8 * g + r, nt, stride=32), :] = t[nt:, :]
+                    table[g, pl.ds(r, nt, stride=8), :] = t[:nt, :]
+                    table[2 + g, pl.ds(r, nt, stride=8), :] = t[nt:, :]
                     r += 1
             if r < 8:
                 for k in range(4):
@@ -122,7 +123,16 @@
             b_rows.append(full)
         n_atoms = count_ref[c]
 
+        def fold(step):
+            at = pl.ds(pl.multiple_of(step * UNROLL, UNROLL), UNROLL)
+            for k in range(3):
+                total = fa[k, pl.ds(0, UNROLL, stride=8), :]
+                for s in range(1, 8):
+                    total = total + fa[k, pl.ds(s, UNROLL, stride=8), :]
+                fb[k, at, :] = total
+
         def atoms(step, carry):
+            fold(step)
             acc = [list(carry[0:3]), list(carry[3:6])]
             e_acc = carry[6]
             for uu in range(UNROLL):
@@ -132,12 +142,12 @@
                 yi = scal_ref[at + slots]
                 zi = scal_ref[at + 2 * slots]
                 qi = scal_ref[at + 3 * slots]
-                ti = pl.multiple_of(type_ref[c * slots + i] * 32, 32)
+                ti = pl.multiple_of(type_ref[c * slots + i] * 8, 8)
                 mine = None
                 for g in range(2):
                     bx, by, bz, bq = b_rows[g]
-                    c12p = table[pl.ds(ti + 8 * g, 8), :]
-                    c6p = table[pl.ds(ti + 16 + 8 * g, 8), :]
+                    c12p = table[g, pl.ds(ti, 8), :]
+                    c6p = table[2 + g, pl.ds(ti, 8), :]
                     dx = bx - xi
                     dy = by - yi
                     dz = bz - zi
@@ -160,11 +170,13 @@
                     acc[g] = [p + q for p, q in zip(acc[g], f)]
                     mine = f if mine is None else [p + q for p, q in zip(mine, f)]
                 for k in range(3):
-                    fa[k, pl.ds(pl.multiple_of(i * 8, 8), 8), :] = mine[k]
+                    fa[k, pl.ds(uu * 8, 8), :] = mine[k]
             return (*acc[0], *acc[1], e_acc)
 
         zero = jnp.zeros((8, slots), jnp.float32)
-        out = lax.fori_loop(0, (n_atoms + UNROLL - 1) // UNROLL, atoms, (zero,) * 6 + (e_sum,))
+        steps = (n_atoms + UNROLL - 1) // UNROLL
+        out = lax.fori_loop(0, steps, atoms, (zero,) * 6 + (e_sum,))
+        fold(steps)
         for g, runs in enumerate(GROUPS):
             r = 0
             for ox, oy, oz, length in runs:
@@ -174,10 +186,7 @@
                 r += length
         mine_lane = wide_lanes == c % slots
         for k in range(3):
-            total = fa[k, pl.ds(0, slots, stride=8), :]
-            for s in range(1, 8):
-                total = total + fa[k, pl.ds(s, slots, stride=8), :]
-            summed = jnp.sum(total, axis=1, keepdims=True)
+            summed = jnp.sum(fb[k, pl.ds(UNROLL, slots), :], axis=1, keepdims=True)
             columns[k, c // slots] = jnp.where(mine_lane, summed, columns[k, c // slots])
         return out[6]
 
@@ -225,8 +234,9 @@
         out_specs=(vm, vm),
         scratch_shapes=[
             pltpu.VMEM((ex * ey, ez, 2 * nt, slots), jnp.float32),
-            pltpu.VMEM(((nt + 1) * 32, slots), jnp.float32),
-            pltpu.VMEM((3, slots * 8, slots), jnp.float32),
+            pltpu.VMEM((4, (nt + 1) * 8, slots), jnp.float32),
+            pltpu.VMEM((3, UNROLL * 8, slots), jnp.float32),
+            pltpu.VMEM((3, UNROLL + slots, slots), jnp.float32),
             pltpu.VMEM((3, parts, slots, slots), jnp.float32),
             pltpu.VMEM((parts * slots, slots), jnp.float32),
         ],

time: 128 us -> 112 us (0.88)
  Pallas kernels: 92.6 us -> 76.5 us
  starting transfers between devices: 15.6 us -> 14 us
  waiting for transfers between devices: 13.1 us -> 14.5 us
    pallas_call x1, Pallas kernels: 92.6 us -> 76.5 us  [on_device(): pl.pallas_call(functools.partial(pair_kernel, cx, cy, cz, nt), out_shape=...]
    ppermute x9, starting transfers between devices: 15.6 us -> 14 us  [shifted(): return lax.ppermute(block, axis, route)]
    ppermute x9, waiting for transfers between devices: 13.1 us -> 14.5 us  [shifted(): return lax.ppermute(block, axis, route)]
where the time goes in v2:
time: 112 us; the launch traced here: 111 us
  Pallas kernels  76.5 us (68%)
  waiting for transfers between devices  14.5 us (13%)
  starting transfers between devices  14 us (12%)
  other arithmetic  3.08 us (3%)
  local copies, waits for them, and re-layouts  2.04 us (2%)
    pallas_call x1, Pallas kernels, on_device(): pl.pallas_call(functools.partial(pair_kernel, cx, cy, cz, nt), out_shape=...  76.5 us
    ppermute x9, waiting for transfers between devices, shifted(): return lax.ppermute(block, axis, route)  14.5 us
    ppermute x9, starting transfers between devices, shifted(): return lax.ppermute(block, axis, route)  14 us
  transfers between devices with their start and end apart: 9, of which 7 were waited for; matrix products, arithmetic and copies ran while one was open for 1% of the time, Pallas kernels for 0%

profile of v2, /device:TPU:0, one launch (start us, length us, event | category | flops | bytes accessed | tf_op | source)
XLA Modules:
  0.0 111.1 jit_solution(10758715788443158780)
XLA Ops:
  0.6 0.8 fusion.5
  1.5 0.8 fusion.4
  2.3 0.1 pad_maximum_fusion.3
  2.4 5.1 %collective-permute-start = (f32[5,1,4,8,128]{4,1,0,3,2:T(1,128)S(1)}, f32[5,1,4,8,128]{4,1,0,3,2:T(1,128)S(1)}, u32[]{:S(2)}, u32[]{:S(2)}) collective-permute-start(f32[5,1,4,8,128]{4,1,0,3,2:T(1,128)S(1)} %pad_maximum_fusion.3), channel_id=1, source_target_pairs={{4,0},{8,4},{12,8},{0,12},{5,1},{9,5},{13,9},{1,13},{6,2},{10,6},{... | collective-permute-start | bytes 245768 | tf_op jit(solution)/shard_map/ppermute | solution.py:27
  7.5 2.1 %collective-permute-done = f32[5,1,4,8,128]{4,1,0,3,2:T(1,128)S(1)} collective-permute-done((f32[5,1,4,8,128]{4,1,0,3,2:T(1,128)S(1)}, f32[5,1,4,8,128]{4,1,0,3,2:T(1,128)S(1)}, u32[]{:S(2)}, u32[]{:S(2)}) %collective-permute-start) | collective-permute-done | bytes 81952 | tf_op jit(solution)/shard_map/ppermute | solution.py:27
  9.6 0.2 pad_maximum_fusion.2
  9.8 1.6 %collective-permute-start.1 = (f32[2,5,2,1,8,128]{5,2,1,4,3,0:T(2,128)S(1)}, f32[2,5,2,1,8,128]{5,2,1,4,3,0:T(2,128)S(1)}, u32[]{:S(2)}, u32[]{:S(2)}) collective-permute-start(f32[2,5,2,1,8,128]{5,2,1,4,3,0:T(2,128)S(1)} %pad_maximum_fusion.4), channel_id=1, source_target_pairs={{2,0},{0,2},{3,1},{1,3},{6,4},{4,6},{7,5},{5,7},{10,8},{8,10},{11,... | collective-permute-start | bytes 245768 | tf_op jit(solution)/shard_map/ppermute | solution.py:27
  11.5 0.1 reshape.261.count_ref
  11.5 2.8 %collective-permute-done.1 = f32[2,5,2,1,8,128]{5,2,1,4,3,0:T(2,128)S(1)} collective-permute-done((f32[2,5,2,1,8,128]{5,2,1,4,3,0:T(2,128)S(1)}, f32[2,5,2,1,8,128]{5,2,1,4,3,0:T(2,128)S(1)}, u32[]{:S(2)}, u32[]{:S(2)}) %collective-permute-start.1) | collective-permute-done | bytes 81952 | tf_op jit(solution)/shard_map/ppermute | solution.py:27
  14.3 0.2 pad_maximum_fusion.1
  14.8 1.2 %collective-permute-done.2 = f32[2,5,2,6,1,128]{5,2,3,1,4,0:T(2,128)S(1)} collective-permute-done((f32[2,5,2,6,1,128]{5,2,3,1,4,0:T(2,128)S(1)}, f32[2,5,2,6,1,128]{5,2,3,1,4,0:T(2,128)S(1)}, u32[]{:S(2)}, u32[]{:S(2)}) %collective-permute-start.2) | collective-permute-done | bytes 61472 | tf_op jit(solution)/shard_map/ppermute | solution.py:27
  16.0 0.1 pad_maximum_fusion.ext_ref
  16.1 0.6 copy-done
  16.8 76.5 %shard_map.82 = (f32[3,12,10,128]{3,2,1,0:T(8,128)S(1)}, f32[8,128]{1,0:T(8,128)S(1)}) custom-call(f32[16384]{0:T(1024)S(1)} %bitcast.50, s32[4096]{0:T(1024)S(1)} %get-tuple-element.94.type_ref, s32[32]{0:T(128)S(1)} %reshape.261.count_ref, f32[5,12,10,128]{3,2,1,0:T(8,128)S(1)} %pad_maximum_fusion.ext_ref, f32[64,64]{1,0:T(8,128)S(1)} %copy-done, ...), custom_call_target="tpu_custom_call" | custom-call | tf_op jit(solution)/shard_map/pallas_call | solution.py:227
  93.6 1.1 %collective-permute-done.3 = f32[73,128]{1,0:T(8,128)S(1)} collective-permute-done((f32[73,128]{1,0:T(8,128)S(1)}, f32[73,128]{1,0:T(8,128)S(1)}, u32[]{:S(2)}, u32[]{:S(2)}) %collective-permute-start.3) | collective-permute-done | bytes 37408 | tf_op jit(solution)/shard_map/ppermute | solution.py:27
  95.0 4.1 %collective-permute-done.4 = f32[97,128]{1,0:T(8,128)S(1)} collective-permute-done((f32[97,128]{1,0:T(8,128)S(1)}, f32[97,128]{1,0:T(8,128)S(1)}, u32[]{:S(2)}, u32[]{:S(2)}) %collective-permute-start.4) | collective-permute-done | bytes 49696 | tf_op jit(solution)/shard_map/ppermute | solution.py:27
  99.1 5.0 %collective-permute-start.7 = (f32[1,128]{1,0:T(1,128)S(1)}, f32[1,128]{1,0:T(1,128)S(1)}, u32[]{:S(2)}, u32[]{:S(2)}) collective-permute-start(f32[1,128]{1,0:T(1,128)S(1)} %slice_add_fusion.4), channel_id=1, source_target_pairs={{8,0},{12,4},{0,8},{4,12},{9,1},{13,5},{1,9},{5,13},{10,2},{14,6},... | collective-permute-start | bytes 1544 | tf_op jit(solution)/shard_map/ppermute | solution.py:27
  104.2 0.1 scatter-add.16
  104.3 0.1 scatter-add.19
  104.5 2.1 %collective-permute-start.5 = (f32[3,1,4,8,128]{4,2,1,0,3:T(4,128)S(1)}, f32[3,1,4,8,128]{4,2,1,0,3:T(4,128)S(1)}, u32[]{:S(2)}, u32[]{:S(2)}) collective-permute-start(f32[3,1,4,8,128]{4,2,1,0,3:T(4,128)S(1)} %slice.293), channel_id=1, source_target_pairs={{12,0},{0,4},{4,8},{8,12},{13,1},{1,5},{5,9},{9,13},{14,2},{2,6},{... | collective-permute-start | bytes 147464 | tf_op jit(solution)/shard_map/ppermute | solution.py:27
  106.6 1.2 %collective-permute-done.8 = f32[1,128]{1,0:T(1,128)S(1)} collective-permute-done((f32[1,128]{1,0:T(1,128)S(1)}, f32[1,128]{1,0:T(1,128)S(1)}, u32[]{:S(2)}, u32[]{:S(2)}) %collective-permute-start.8) | collective-permute-done | bytes 544 | tf_op jit(solution)/shard_map/ppermute | solution.py:27
  107.7 0.6 add_reduce_fusion
  108.3 2.1 %collective-permute-done.5 = f32[3,1,4,8,128]{4,2,1,0,3:T(4,128)S(1)} collective-permute-done((f32[3,1,4,8,128]{4,2,1,0,3:T(4,128)S(1)}, f32[3,1,4,8,128]{4,2,1,0,3:T(4,128)S(1)}, u32[]{:S(2)}, u32[]{:S(2)}) %collective-permute-start.5) | collective-permute-done | bytes 49184 | tf_op jit(solution)/shard_map/ppermute | solution.py:27
  110.5 0.6 copy.41
  (52 shorter events, 1.0 us)
Async XLA Ops:
  0.6 1.6 %copy-start.2 = (f32[1,4,8,3,128]{4,2,3,1,0:T(8,128)S(1)}, f32[1,4,8,3,128]{4,2,3,1,0:T(8,128)}, u32[]{:S(2)}) copy-start(f32[1,4,8,3,128]{4,2,3,1,0:T(8,128)} %param.18) | copy-start | bytes 147460
  0.6 0.8 copy-start.4
  2.4 7.2 %collective-permute-start = (f32[5,1,4,8,128]{4,1,0,3,2:T(1,128)S(1)}, f32[5,1,4,8,128]{4,1,0,3,2:T(1,128)S(1)}, u32[]{:S(2)}, u32[]{:S(2)}) collective-permute-start(f32[5,1,4,8,128]{4,1,0,3,2:T(1,128)S(1)} %pad_maximum_fusion.3), channel_id=1, source_target_pairs={{4,0},{8,4},{12,8},{0,12},{5,1},{9,5},{13,9},{1,13},{6,2},{10,6},{... | collective-permute-start | bytes 245768 | tf_op jit(solution)/shard_map/ppermute | solution.py:27
  9.8 1.6 %copy-start.3 = (f32[1,4,8,128]{3,2,1,0:T(8,128)S(1)}, f32[1,4,8,128]{3,2,1,0:T(8,128)}, u32[]{:S(2)}) copy-start(f32[1,4,8,128]{3,2,1,0:T(8,128)} %param.19) | copy-start | bytes 49156
  9.8 4.5 %collective-permute-start.1 = (f32[2,5,2,1,8,128]{5,2,1,4,3,0:T(2,128)S(1)}, f32[2,5,2,1,8,128]{5,2,1,4,3,0:T(2,128)S(1)}, u32[]{:S(2)}, u32[]{:S(2)}) collective-permute-start(f32[2,5,2,1,8,128]{5,2,1,4,3,0:T(2,128)S(1)} %pad_maximum_fusion.4), channel_id=1, source_target_pairs={{2,0},{0,2},{3,1},{1,3},{6,4},{4,6},{7,5},{5,7},{10,8},{8,10},{11,... | collective-permute-start | bytes 245768 | tf_op jit(solution)/shard_map/ppermute | solution.py:27
  14.6 1.3 %collective-permute-start.2 = (f32[2,5,2,6,1,128]{5,2,3,1,4,0:T(2,128)S(1)}, f32[2,5,2,6,1,128]{5,2,3,1,4,0:T(2,128)S(1)}, u32[]{:S(2)}, u32[]{:S(2)}) collective-permute-start(f32[2,5,2,6,1,128]{5,2,3,1,4,0:T(2,128)S(1)} %pad_maximum_fusion.6), channel_id=1, source_target_pairs={{1,0},{0,1},{3,2},{2,3},{5,4},{4,5},{7,6},{6,7},{9,8},{8,9},{11,10... | collective-permute-start | bytes 184328 | tf_op jit(solution)/shard_map/ppermute | solution.py:27
  16.0 0.8 copy-start
  16.0 0.8 copy-start.1
  93.4 1.3 %collective-permute-start.3 = (f32[73,128]{1,0:T(8,128)S(1)}, f32[73,128]{1,0:T(8,128)S(1)}, u32[]{:S(2)}, u32[]{:S(2)}) collective-permute-start(f32[73,128]{1,0:T(8,128)S(1)} %pad_maximum_fusion.9), channel_id=1, source_target_pairs={{1,0},{0,1},{3,2},{2,3},{5,4},{4,5},{7,6},{6,7},{9,8},{8,9},{11,10... | collective-permute-start | bytes 112136 | tf_op jit(solution)/shard_map/ppermute | solution.py:27
  94.9 4.2 %collective-permute-start.4 = (f32[97,128]{1,0:T(8,128)S(1)}, f32[97,128]{1,0:T(8,128)S(1)}, u32[]{:S(2)}, u32[]{:S(2)}) collective-permute-start(f32[97,128]{1,0:T(8,128)S(1)} %pad_maximum_fusion.7), channel_id=1, source_target_pairs={{2,0},{0,2},{3,1},{1,3},{6,4},{4,6},{7,5},{5,7},{10,8},{8,10},{11,... | collective-permute-start | bytes 149000 | tf_op jit(solution)/shard_map/ppermute | solution.py:27
  99.1 7.5 %collective-permute-start.6 = (f32[1,128]{1,0:T(1,128)S(1)}, f32[1,128]{1,0:T(1,128)S(1)}, u32[]{:S(2)}, u32[]{:S(2)}) collective-permute-start(f32[1,128]{1,0:T(1,128)S(1)} %slice_add_fusion.4), channel_id=1, source_target_pairs={{12,0},{0,4},{4,8},{8,12},{13,1},{1,5},{5,9},{9,13},{14,2},{2,6},{... | collective-permute-start | bytes 1544 | tf_op jit(solution)/shard_map/ppermute | solution.py:27
  99.1 7.5 %collective-permute-start.7 = (f32[1,128]{1,0:T(1,128)S(1)}, f32[1,128]{1,0:T(1,128)S(1)}, u32[]{:S(2)}, u32[]{:S(2)}) collective-permute-start(f32[1,128]{1,0:T(1,128)S(1)} %slice_add_fusion.4), channel_id=1, source_target_pairs={{8,0},{12,4},{0,8},{4,12},{9,1},{13,5},{1,9},{5,13},{10,2},{14,6},... | collective-permute-start | bytes 1544 | tf_op jit(solution)/shard_map/ppermute | solution.py:27
  104.1 3.6 %collective-permute-start.8 = (f32[1,128]{1,0:T(1,128)S(1)}, f32[1,128]{1,0:T(1,128)S(1)}, u32[]{:S(2)}, u32[]{:S(2)}) collective-permute-start(f32[1,128]{1,0:T(1,128)S(1)} %slice_add_fusion.4), channel_id=1, source_target_pairs={{4,0},{8,4},{12,8},{0,12},{5,1},{9,5},{13,9},{1,13},{6,2},{10,6},{... | collective-permute-start | bytes 1544 | tf_op jit(solution)/shard_map/ppermute | solution.py:27
  104.5 5.9 %collective-permute-start.5 = (f32[3,1,4,8,128]{4,2,1,0,3:T(4,128)S(1)}, f32[3,1,4,8,128]{4,2,1,0,3:T(4,128)S(1)}, u32[]{:S(2)}, u32[]{:S(2)}) collective-permute-start(f32[3,1,4,8,128]{4,2,1,0,3:T(4,128)S(1)} %slice.293), channel_id=1, source_target_pairs={{12,0},{0,4},{4,8},{8,12},{13,1},{1,5},{5,9},{9,13},{14,2},{2,6},{... | collective-permute-start | bytes 147464 | tf_op jit(solution)/shard_map/ppermute | solution.py:27

commit v3 on v2

--- a/solution.py
+++ b/solution.py
@@ -119,7 +119,6 @@
                             off = jnp.where(rows == r, jnp.float32(o * CELL_EDGE), off)
                         r += 1
                 full[k] = full[k] + off
-            full[3] = full[3] * ENERGY_UNIT
             b_rows.append(full)
         n_atoms = count_ref[c]
 
@@ -213,7 +212,7 @@
     local = jnp.concatenate(
         [jnp.moveaxis(coords, 3, 0), charge[None], kind.astype(jnp.float32)[None]], axis=0
     )
-    scal = jnp.concatenate([coords, charge[..., None, :]], axis=3).reshape(-1)
+    scal = jnp.concatenate([coords, ENERGY_UNIT * charge[..., None, :]], axis=3).reshape(-1)
     up = shifted(local[:, :1], "gx", -1)
     ext = jnp.concatenate([local, up], axis=1)
     above, below = from_both(ext[:, :, :1], ext[:, :, -1:], "gy")
@@ -244,13 +243,14 @@
     )(scal, kind.reshape(-1), counts.reshape(-1), ext.reshape(5, ex * ey, ez, slots), c6_table, c12_table)
     energy = jnp.sum(energy, axis=0, keepdims=True)
     forces = forces.reshape(3, ex, ey, ez, slots)
-    low, high, energy = returned(forces[:, :, :, :1], forces[:, :, :, -1:], energy, "gz")
+    low, high = from_both(forces[:, :, :, :1], forces[:, :, :, -1:], "gz")
+    energy = ring_sum(energy, "gx")
     forces = forces[:, :, :, 1:-1].at[:, :, :, -1:].add(low).at[:, :, :, :1].add(high)
     low, high, energy = returned(forces[:, :, :1], forces[:, :, -1:], energy, "gy")
     forces = forces[:, :, 1:-1].at[:, :, -1:].add(low).at[:, :, :1].add(high)
     back = shifted(forces[:, cx:], "gx", 1)
     forces = forces[:, :cx].at[:, :1].add(back)
-    energy = jnp.sum(ring_sum(energy, "gx"))
+    energy = jnp.sum(ring_sum(energy, "gz"))
     return jnp.moveaxis(forces, 0, 3), energy.reshape(1)
 
 

time: 112 us -> 111 us (level); the launches traced: 111 us -> 112 us
  Pallas kernels: 76.5 us -> 71.4 us
  starting transfers between devices: 14 us -> 18 us
  waiting for transfers between devices: 14.5 us -> 16.7 us
    pallas_call x1, Pallas kernels: 76.5 us -> 71.4 us  [on_device(): pl.pallas_call(functools.partial(pair_kernel, cx, cy, cz, nt), out_shape=...]
    ppermute x9 -> x10, starting transfers between devices: 14 us -> 18 us  [shifted(): return lax.ppermute(block, axis, route)]
    ppermute x9 -> x10, waiting for transfers between devices: 14.5 us -> 16.7 us  [shifted(): return lax.ppermute(block, axis, route)]
  transfers between devices with their start and end apart: 9 -> 10, of which waited for: 7 -> 9; matrix products, arithmetic and copies ran while one was open for 1% -> 1% of each run, Pallas kernels for 0% -> 0%
where the time goes in v3:
time: 111 us; the launch traced here: 112 us
  Pallas kernels  71.4 us (64%)
  starting transfers between devices  18 us (16%)
  waiting for transfers between devices  16.7 us (15%)
  other arithmetic  3.02 us (3%)
  local copies, waits for them, and re-layouts  1.81 us (2%)
    pallas_call x1, Pallas kernels, on_device(): pl.pallas_call(functools.partial(pair_kernel, cx, cy, cz, nt), out_shape=...  71.4 us
    ppermute x10, starting transfers between devices, shifted(): return lax.ppermute(block, axis, route)  18 us
    ppermute x10, waiting for transfers between devices, shifted(): return lax.ppermute(block, axis, route)  16.7 us
  transfers between devices with their start and end apart: 10, of which 9 were waited for; matrix products, arithmetic and copies ran while one was open for 1% of the time, Pallas kernels for 0%

profile of v3, /device:TPU:0, one launch (start us, length us, event | category | flops | bytes accessed | tf_op | source)
XLA Modules:
  0.0 111.9 jit_solution(12709060731259322559)
XLA Ops:
  0.6 0.8 multiply_bitcast_fusion
  1.5 0.8 fusion.9
  2.4 5.1 %collective-permute-start = (f32[5,1,4,8,128]{4,1,0,3,2:T(1,128)S(1)}, f32[5,1,4,8,128]{4,1,0,3,2:T(1,128)S(1)}, u32[]{:S(2)}, u32[]{:S(2)}) collective-permute-start(f32[5,1,4,8,128]{4,1,0,3,2:T(1,128)S(1)} %pad_maximum_fusion.3), channel_id=1, source_target_pairs={{4,0},{8,4},{12,8},{0,12},{5,1},{9,5},{13,9},{1,13},{6,2},{10,6},{... | collective-permute-start | bytes 245768 | tf_op jit(solution)/shard_map/ppermute | solution.py:27
  7.5 2.1 %collective-permute-done = f32[5,1,4,8,128]{4,1,0,3,2:T(1,128)S(1)} collective-permute-done((f32[5,1,4,8,128]{4,1,0,3,2:T(1,128)S(1)}, f32[5,1,4,8,128]{4,1,0,3,2:T(1,128)S(1)}, u32[]{:S(2)}, u32[]{:S(2)}) %collective-permute-start) | collective-permute-done | bytes 81952 | tf_op jit(solution)/shard_map/ppermute | solution.py:27
  9.6 0.2 pad_maximum_fusion.2
  9.8 1.6 %collective-permute-start.1 = (f32[2,5,2,1,8,128]{5,2,1,4,3,0:T(2,128)S(1)}, f32[2,5,2,1,8,128]{5,2,1,4,3,0:T(2,128)S(1)}, u32[]{:S(2)}, u32[]{:S(2)}) collective-permute-start(f32[2,5,2,1,8,128]{5,2,1,4,3,0:T(2,128)S(1)} %pad_maximum_fusion.4), channel_id=1, source_target_pairs={{2,0},{0,2},{3,1},{1,3},{6,4},{4,6},{7,5},{5,7},{10,8},{8,10},{11,... | collective-permute-start | bytes 245768 | tf_op jit(solution)/shard_map/ppermute | solution.py:27
  11.4 2.9 %collective-permute-done.1 = f32[2,5,2,1,8,128]{5,2,1,4,3,0:T(2,128)S(1)} collective-permute-done((f32[2,5,2,1,8,128]{5,2,1,4,3,0:T(2,128)S(1)}, f32[2,5,2,1,8,128]{5,2,1,4,3,0:T(2,128)S(1)}, u32[]{:S(2)}, u32[]{:S(2)}) %collective-permute-start.1) | collective-permute-done | bytes 81952 | tf_op jit(solution)/shard_map/ppermute | solution.py:27
  14.3 0.2 pad_maximum_fusion.1
  14.7 1.2 %collective-permute-done.2 = f32[2,5,2,6,1,128]{5,2,3,1,4,0:T(2,128)S(1)} collective-permute-done((f32[2,5,2,6,1,128]{5,2,3,1,4,0:T(2,128)S(1)}, f32[2,5,2,6,1,128]{5,2,3,1,4,0:T(2,128)S(1)}, u32[]{:S(2)}, u32[]{:S(2)}) %collective-permute-start.2) | collective-permute-done | bytes 61472 | tf_op jit(solution)/shard_map/ppermute | solution.py:27
  16.0 0.1 pad_maximum_fusion.ext_ref
  16.1 0.6 copy-done
  16.8 71.4 %shard_map.82 = (f32[3,12,10,128]{3,2,1,0:T(8,128)S(1)}, f32[8,128]{1,0:T(8,128)S(1)}) custom-call(f32[16384]{0:T(1024)S(1)} %bitcast.63, s32[4096]{0:T(1024)S(1)} %get-tuple-element.96.type_ref, s32[32]{0:T(128)S(1)} %reshape.267.count_ref, f32[5,12,10,128]{3,2,1,0:T(8,128)S(1)} %pad_maximum_fusion.ext_ref, f32[64,64]{1,0:T(8,128)S(1)} %copy-done, ...), custom_call_target="tpu_custom_call" | custom-call | tf_op jit(solution)/shard_map/pallas_call | solution.py:226
  88.2 1.8 %collective-permute-start.4 = (f32[1,128]{1,0:T(1,128)S(1)}, f32[1,128]{1,0:T(1,128)S(1)}, u32[]{:S(2)}, u32[]{:S(2)}) collective-permute-start(f32[1,128]{1,0:T(1,128)S(1)} %bitcast.83), channel_id=1, source_target_pairs={{12,0},{0,4},{4,8},{8,12},{13,1},{1,5},{5,9},{9,13},{14,2},{2,6},{... | collective-permute-start | bytes 1544 | tf_op jit(solution)/shard_map/ppermute | solution.py:27
  90.0 6.9 %collective-permute-start.5 = (f32[1,128]{1,0:T(1,128)S(1)}, f32[1,128]{1,0:T(1,128)S(1)}, u32[]{:S(2)}, u32[]{:S(2)}) collective-permute-start(f32[1,128]{1,0:T(1,128)S(1)} %bitcast.84), channel_id=1, source_target_pairs={{8,0},{12,4},{0,8},{4,12},{9,1},{13,5},{1,9},{5,13},{10,2},{14,6},... | collective-permute-start | bytes 1544 | tf_op jit(solution)/shard_map/ppermute | solution.py:27
  97.2 0.7 collective-permute-done.4
  97.9 0.6 collective-permute-done.5
  98.4 2.0 %collective-permute-done.6 = f32[1,128]{1,0:T(1,128)S(1)} collective-permute-done((f32[1,128]{1,0:T(1,128)S(1)}, f32[1,128]{1,0:T(1,128)S(1)}, u32[]{:S(2)}, u32[]{:S(2)}) %collective-permute-start.6) | collective-permute-done | bytes 544 | tf_op jit(solution)/shard_map/ppermute | solution.py:27
  100.6 2.4 %collective-permute-start.7 = (f32[97,128]{1,0:T(8,128)S(1)}, f32[97,128]{1,0:T(8,128)S(1)}, u32[]{:S(2)}, u32[]{:S(2)}) collective-permute-start(f32[97,128]{1,0:T(8,128)S(1)} %pad_maximum_fusion.7), channel_id=1, source_target_pairs={{2,0},{0,2},{3,1},{1,3},{6,4},{4,6},{7,5},{5,7},{10,8},{8,10},{11,... | collective-permute-start | bytes 149000 | tf_op jit(solution)/shard_map/ppermute | solution.py:27
  103.0 2.1 %collective-permute-done.7 = f32[97,128]{1,0:T(8,128)S(1)} collective-permute-done((f32[97,128]{1,0:T(8,128)S(1)}, f32[97,128]{1,0:T(8,128)S(1)}, u32[]{:S(2)}, u32[]{:S(2)}) %collective-permute-start.7) | collective-permute-done | bytes 49696 | tf_op jit(solution)/shard_map/ppermute | solution.py:27
  105.2 0.1 collective-permute-start.8
  105.4 0.9 collective-permute-done.9
  106.3 0.6 add_reduce_fusion
  106.9 4.4 %collective-permute-done.8 = f32[3,1,4,8,128]{4,1,2,0,3:T(1,128)S(1)} collective-permute-done((f32[3,1,4,8,128]{4,1,2,0,3:T(1,128)S(1)}, f32[3,1,4,8,128]{4,1,2,0,3:T(1,128)S(1)}, u32[]{:S(2)}, u32[]{:S(2)}) %collective-permute-start.8) | collective-permute-done | bytes 49184 | tf_op jit(solution)/shard_map/ppermute | solution.py:27
  111.3 0.6 copy.59
  (46 shorter events, 1.1 us)
Async XLA Ops:
  0.6 0.8 copy-start.3
  0.6 1.6 %copy-start.2 = (f32[1,4,8,3,128]{4,2,3,1,0:T(8,128)S(1)}, f32[1,4,8,3,128]{4,2,3,1,0:T(8,128)}, u32[]{:S(2)}) copy-start(f32[1,4,8,3,128]{4,2,3,1,0:T(8,128)} %param.18) | copy-start | bytes 147460
  2.4 7.2 %collective-permute-start = (f32[5,1,4,8,128]{4,1,0,3,2:T(1,128)S(1)}, f32[5,1,4,8,128]{4,1,0,3,2:T(1,128)S(1)}, u32[]{:S(2)}, u32[]{:S(2)}) collective-permute-start(f32[5,1,4,8,128]{4,1,0,3,2:T(1,128)S(1)} %pad_maximum_fusion.3), channel_id=1, source_target_pairs={{4,0},{8,4},{12,8},{0,12},{5,1},{9,5},{13,9},{1,13},{6,2},{10,6},{... | collective-permute-start | bytes 245768 | tf_op jit(solution)/shard_map/ppermute | solution.py:27
  9.8 4.5 %collective-permute-start.1 = (f32[2,5,2,1,8,128]{5,2,1,4,3,0:T(2,128)S(1)}, f32[2,5,2,1,8,128]{5,2,1,4,3,0:T(2,128)S(1)}, u32[]{:S(2)}, u32[]{:S(2)}) collective-permute-start(f32[2,5,2,1,8,128]{5,2,1,4,3,0:T(2,128)S(1)} %pad_maximum_fusion.4), channel_id=1, source_target_pairs={{2,0},{0,2},{3,1},{1,3},{6,4},{4,6},{7,5},{5,7},{10,8},{8,10},{11,... | collective-permute-start | bytes 245768 | tf_op jit(solution)/shard_map/ppermute | solution.py:27
  14.6 1.3 %collective-permute-start.2 = (f32[2,5,2,6,1,128]{5,2,3,1,4,0:T(2,128)S(1)}, f32[2,5,2,6,1,128]{5,2,3,1,4,0:T(2,128)S(1)}, u32[]{:S(2)}, u32[]{:S(2)}) collective-permute-start(f32[2,5,2,6,1,128]{5,2,3,1,4,0:T(2,128)S(1)} %pad_maximum_fusion.6), channel_id=1, source_target_pairs={{1,0},{0,1},{3,2},{2,3},{5,4},{4,5},{7,6},{6,7},{9,8},{8,9},{11,10... | collective-permute-start | bytes 184328 | tf_op jit(solution)/shard_map/ppermute | solution.py:27
  16.0 0.8 copy-start
  16.0 0.8 copy-start.1
  88.2 9.7 %collective-permute-start.4 = (f32[1,128]{1,0:T(1,128)S(1)}, f32[1,128]{1,0:T(1,128)S(1)}, u32[]{:S(2)}, u32[]{:S(2)}) collective-permute-start(f32[1,128]{1,0:T(1,128)S(1)} %bitcast.83), channel_id=1, source_target_pairs={{12,0},{0,4},{4,8},{8,12},{13,1},{1,5},{5,9},{9,13},{14,2},{2,6},{... | collective-permute-start | bytes 1544 | tf_op jit(solution)/shard_map/ppermute | solution.py:27
  90.0 8.4 %collective-permute-start.5 = (f32[1,128]{1,0:T(1,128)S(1)}, f32[1,128]{1,0:T(1,128)S(1)}, u32[]{:S(2)}, u32[]{:S(2)}) collective-permute-start(f32[1,128]{1,0:T(1,128)S(1)} %bitcast.84), channel_id=1, source_target_pairs={{8,0},{12,4},{0,8},{4,12},{9,1},{13,5},{1,9},{5,13},{10,2},{14,6},... | collective-permute-start | bytes 1544 | tf_op jit(solution)/shard_map/ppermute | solution.py:27
  96.9 3.6 %collective-permute-start.6 = (f32[1,128]{1,0:T(1,128)S(1)}, f32[1,128]{1,0:T(1,128)S(1)}, u32[]{:S(2)}, u32[]{:S(2)}) collective-permute-start(f32[1,128]{1,0:T(1,128)S(1)} %bitcast.85), channel_id=1, source_target_pairs={{4,0},{8,4},{12,8},{0,12},{5,1},{9,5},{13,9},{1,13},{6,2},{10,6},{... | collective-permute-start | bytes 1544 | tf_op jit(solution)/shard_map/ppermute | solution.py:27
  97.0 3.5 %collective-permute-start.3 = (f32[2,3,2,6,1,128]{5,2,3,1,4,0:T(2,128)S(1)}, f32[2,3,2,6,1,128]{5,2,3,1,4,0:T(2,128)S(1)}, u32[]{:S(2)}, u32[]{:S(2)}) collective-permute-start(f32[2,3,2,6,1,128]{5,2,3,1,4,0:T(2,128)S(1)} %pad_maximum_fusion.9), channel_id=1, source_target_pairs={{1,0},{0,1},{3,2},{2,3},{5,4},{4,5},{7,6},{6,7},{9,8},{8,9},{11,10... | collective-permute-start | bytes 110600 | tf_op jit(solution)/shard_map/ppermute | solution.py:27
  100.6 4.5 %collective-permute-start.7 = (f32[97,128]{1,0:T(8,128)S(1)}, f32[97,128]{1,0:T(8,128)S(1)}, u32[]{:S(2)}, u32[]{:S(2)}) collective-permute-start(f32[97,128]{1,0:T(8,128)S(1)} %pad_maximum_fusion.7), channel_id=1, source_target_pairs={{2,0},{0,2},{3,1},{1,3},{6,4},{4,6},{7,5},{5,7},{10,8},{8,10},{11,... | collective-permute-start | bytes 149000 | tf_op jit(solution)/shard_map/ppermute | solution.py:27
  105.1 1.2 %collective-permute-start.9 = (f32[1,128]{1,0:T(1,128)S(1)}, f32[1,128]{1,0:T(1,128)S(1)}, u32[]{:S(2)}, u32[]{:S(2)}) collective-permute-start(f32[1,128]{1,0:T(1,128)S(1)} %slice_add_fusion.3), channel_id=1, source_target_pairs={{1,0},{0,1},{3,2},{2,3},{5,4},{4,5},{7,6},{6,7},{9,8},{8,9},{11,10... | collective-permute-start | bytes 1544 | tf_op jit(solution)/shard_map/ppermute | solution.py:27
  105.2 6.0 %collective-permute-start.8 = (f32[3,1,4,8,128]{4,1,2,0,3:T(1,128)S(1)}, f32[3,1,4,8,128]{4,1,2,0,3:T(1,128)S(1)}, u32[]{:S(2)}, u32[]{:S(2)}) collective-permute-start(f32[3,1,4,8,128]{4,1,2,0,3:T(1,128)S(1)} %slice.283), channel_id=1, source_target_pairs={{12,0},{0,4},{4,8},{8,12},{13,1},{1,5},{5,9},{9,13},{14,2},{2,6},{... | collective-permute-start | bytes 147464 | tf_op jit(solution)/shard_map/ppermute | solution.py:27
